TPU v7x, 32 devices: a whole 2x2x4 slice. The times are simulated.
32 devices in a mesh: blk: 16 (over z, y, x), col: 2 (over core).
Axes of the slice: x: 2, y: 2, z: 4, core: 2. Of those that a mesh axis runs over, the one named last changes fastest.
Arguments:
- queries: bfloat16 [128, 16384], P('blk', 'col'), may hold values from -6 to 6
- factor: bfloat16 [16384, 1024], P('col', 'blk'), may hold values from -0.046875 to 0.046875
- eigenvalues: float32 [1024], replicated, may hold values from 0.05 to 20
- damping: float32 [1], replicated, may hold values from 0.5 to 2
- train_rows: bfloat16 [16384, 16384], P('blk', 'col'), may hold values from -0.046875 to 0.046875
Outputs:
- scores: bfloat16 [128, 16384], P('col', 'blk')
All inputs are finite; a program needn't handle non-finite values.
Results may differ from a plain program's by a relative error of at most 0.0049.
Values may be sent and summed in bfloat16 or wider, within the bound.
A program may use at most 64 MiB of HBM per device.

v0:
```python
import jax
import jax.numpy as jnp
from jax import lax
from jax.sharding import PartitionSpec as P


def row_scores(block_rows, train_rows):
    return jnp.einsum("qk,nk->qn", block_rows, train_rows, preferred_element_type=jnp.float32)


def per_device(queries, factor, eigenvalues, damping, train_rows):
    damp_value = damping[0]
    weights = eigenvalues / (eigenvalues + damp_value)
    rank_slice = factor.shape[1]
    every_query = lax.all_gather(queries, "blk", axis=0, tiled=True)
    partial_value = jnp.dot(every_query, factor, preferred_element_type=jnp.float32)
    coefficient = lax.psum(partial_value, "col")
    slice_weights = lax.dynamic_slice_in_dim(
        weights, lax.axis_index("blk") * rank_slice, rank_slice
    )
    scaled = coefficient * slice_weights[None, :]
    correction_part = jnp.dot(scaled, factor.astype(jnp.float32).T, precision=lax.Precision.HIGHEST)
    correction = lax.psum(correction_part, "blk")
    pre_all = ((every_query.astype(jnp.float32) - correction) / damp_value).astype(jnp.bfloat16)
    partial_scores = row_scores(pre_all, train_rows)
    scores = lax.psum_scatter(partial_scores, "col", scatter_dimension=0, tiled=True)
    return scores.astype(jnp.bfloat16)


def solution(mesh):
    in_specs = (P("blk", "col"), P("col", "blk"), P(), P(), P("blk", "col"))
    out_specs = P("col", "blk")
    return jax.shard_map(
        per_device, mesh=mesh, in_specs=in_specs, out_specs=out_specs, check_vma=False
    )
```

profile of v0, /device:TPU:0, one launch (start us, length us, event | category | flops | bytes accessed | tf_op | source)
XLA Modules:
  0.0 279.0 jit_solution(8576192515819052841)
XLA Ops:
  6.5 0.0 copy-start
  6.5 0.0 all-gather.2.cloned.1.call-start
  6.5 0.7 all-gather.2.cloned.1.call-update
  7.3 0.0 all-reduce.2.cloned.1.call-start
  8.0 0.7 add_divide_fusion
  8.6 0.1 dynamic_slice.3
  8.7 64.5 %all-gather.2.cloned.1.call-done = bf16[128,8192]{1,0:T(8,128)(2,1)} async-done(((bf16[8,8192]{1,0:T(8,128)(2,1)}), bf16[128,8192]{1,0:T(8,128)(2,1)}) %all-gather.2.cloned.1.call-update) | async-done | bytes 2097168 | tf_op jit(solution)/shard_map/all_gather | solution.py:15
  73.2 0.0 copy-done
  73.2 2.3 fusion.5
  75.5 3.6 %psum.14 = f32[128,64]{1,0:T(8,128)S(1)} all-reduce(f32[128,64]{1,0:T(8,128)S(1)} %fusion.5), channel_id=1, replica_groups=mesh['blk'=16,'col'=2] {'col'}, use_global_device_ids=true, to_apply=%region_0.0 | all-reduce | flops 8192 | bytes 65536 | tf_op jit(solution)/shard_map/psum | solution.py:17
  79.1 0.0 copy-start.1
  79.1 3.7 %fusion.2 = f32[128,8192]{1,0:T(8,128)} fusion(bf16[8192,64]{0,1:T(8,128)(2,1)S(1)} %copy-done, f32[128,64]{1,0:T(8,128)S(1)} %psum.14, f32[64]{0:T(128)S(1)} %dynamic_slice.3), kind=kOutput, calls=%fused_computation.3 | convolution fusion | flops 805314560 | bytes 5275904 | tf_op jit(solution)/shard_map/dot_general | solution.py:22
  82.9 0.0 all-reduce.2.cloned.1.call-update
  82.9 0.0 reduce-scatter.2.cloned.1.call-start
  83.0 167.2 %all-reduce.2.cloned.1.call-done = f32[128,8192]{1,0:T(8,128)} async-done(((f32[128,8192]{1,0:T(8,128)}), f32[128,8192]{1,0:T(8,128)}) %all-reduce.2.cloned.1.call-update) | async-done | bytes 4194320 | tf_op jit(solution)/shard_map/psum | solution.py:23
  250.2 0.0 copy-done.1
  250.2 13.5 %fusion = f32[128,1024]{1,0:T(8,128)} fusion(bf16[1024,8192]{1,0:T(8,128)(2,1)} %param.9, f32[128,8192]{1,0:T(8,128)} %all-reduce.2.cloned.1.call-done, bf16[128,8192]{1,0:T(8,128)(2,1)S(1)} %copy-done.1, f32[]{:T(128)} %bitcast.6), kind=kOutput, calls=%fused_computation.1 | convolution fusion | flops 2151677952 | bytes 23592964 | tf_op jit(solution)/shard_map/qk,nk->qn/dot_general | solution.py:8
  263.7 0.0 reduce-scatter.2.cloned.1.call-update
  263.7 7.1 %reduce-scatter.2.cloned.1.call-done = f32[64,1024]{1,0:T(8,128)} async-done(((f32[128,1024]{1,0:T(8,128)}), f32[64,1024]{1,0:T(8,128)}) %reduce-scatter.2.cloned.1.call-update) | async-done | bytes 262160 | tf_op jit(solution)/shard_map/reduce_scatter | solution.py:26
  270.8 1.6 convert_element_type.12
Async XLA Ops:
  6.5 66.7 %copy-start = (bf16[8192,64]{0,1:T(8,128)(2,1)S(1)}, bf16[8192,64]{0,1:T(8,128)(2,1)}, u32[]{:S(2)}) copy-start(bf16[8192,64]{0,1:T(8,128)(2,1)} %param.6) | copy-start | bytes 3145732
  6.5 66.7 %all-gather.2.cloned.1.call-start = ((), (), s32[]{:S(2)}) async-start(), calls=%async_computation.1 | async-start | bytes 2228224 | tf_op jit(solution)/shard_map/all_gather | solution.py:15
  7.3 242.9 %all-reduce.2.cloned.1.call-start = ((), (), s32[]{:S(2)}) async-start(), calls=%async_computation.2 | async-start | bytes 8388608 | tf_op jit(solution)/shard_map/psum | solution.py:23
  79.1 171.0 %copy-start.1 = (bf16[128,8192]{1,0:T(8,128)(2,1)S(1)}, bf16[128,8192]{1,0:T(8,128)(2,1)}, u32[]{:S(2)}) copy-start(bf16[128,8192]{1,0:T(8,128)(2,1)} %all-gather.2.cloned.1.call-done) | copy-start | bytes 6291460
  82.9 187.9 %reduce-scatter.2.cloned.1.call-start = ((), (), s32[]{:S(2)}) async-start(), calls=%async_computation.3 | async-start | bytes 786432 | tf_op jit(solution)/shard_map/reduce_scatter | solution.py:26
Sparse Core Ops, SparseCore 0:
  10.1 63.0 all-gather.1
  83.0 167.0 all-reduce.1
  263.8 6.9 reduce-scatter.1
where the time goes:
time: 279 us
  waiting for transfers between devices  240 us (86%)
  matrix products  19.5 us (7%)
  between operations  13.8 us (5%)
  blocking collectives  3.59 us (1%)
    psum x1, waiting for transfers between devices, per_device(): correction = lax.psum(correction_part, 'blk')  167 us
    all_gather x1, waiting for transfers between devices, per_device(): every_query = lax.all_gather(queries, 'blk', axis=0, tiled=True)  64.5 us
    dot_general x1, matrix products, row_scores(): jnp.einsum('qk,nk->qn', block_rows, train_rows, preferred_element_type=jn...  13.5 us
    reduce_scatter x1, waiting for transfers between devices, per_device(): lax.psum_scatter(partial_scores, 'col', scatter_dimension=0, tiled=True)  7.13 us
  transfers between devices with their start and end apart: 3, of which 3 were waited for; matrix products, arithmetic and copies ran while one was open for 0% of the time, Pallas kernels for 0%

commit v1 on v0

--- a/solution.py
+++ b/solution.py
@@ -20,7 +20,13 @@
     )
     scaled = coefficient * slice_weights[None, :]
     correction_part = jnp.dot(scaled, factor.astype(jnp.float32).T, precision=lax.Precision.HIGHEST)
-    correction = lax.psum(correction_part, "blk")
+    size = lax.axis_size("blk")
+    correction, far = (correction_part, 1)
+    while far < size:
+        correction = correction + lax.ppermute(
+            correction, "blk", [(i, i ^ far) for i in range(size)]
+        )
+        far = 2 * far
     pre_all = ((every_query.astype(jnp.float32) - correction) / damp_value).astype(jnp.bfloat16)
     partial_scores = row_scores(pre_all, train_rows)
     scores = lax.psum_scatter(partial_scores, "col", scatter_dimension=0, tiled=True)

time: 279 us -> 569 us (2.04)
  waiting for transfers between devices: 240 us -> 523 us
  starting transfers between devices: 0.08 us -> 6.16 us
    ppermute x0 -> x4, waiting for transfers between devices: none -> 451 us  [per_device(): lax.ppermute(correction, 'blk', [(i, i ^ far) for i in range(size)])]
    psum x1 -> x0, waiting for transfers between devices: 167 us -> none  [per_device(): correction = lax.psum(correction_part, 'blk')]
    ppermute x0 -> x4, starting transfers between devices: none -> 6.12 us  [per_device(): lax.ppermute(correction, 'blk', [(i, i ^ far) for i in range(size)])]
  transfers between devices with their start and end apart: 3 -> 6, of which waited for: 3 -> 6; matrix products, arithmetic and copies ran while one was open for 0% -> 0% of each run, Pallas kernels for 0% -> 0%
where the time goes in v1:
time: 569 us; the launch traced here: 568 us
  waiting for transfers between devices  523 us (92%)
  matrix products  15.5 us (3%)
  between operations  14.1 us (2%)
  starting transfers between devices  6.16 us (1%)
    ppermute x4, waiting for transfers between devices, per_device(): lax.ppermute(correction, 'blk', [(i, i ^ far) for i in range(size)])  451 us
    all_gather x1, waiting for transfers between devices, per_device(): every_query = lax.all_gather(queries, 'blk', axis=0, tiled=True)  64.5 us
    dot_general x1, matrix products, row_scores(): jnp.einsum('qk,nk->qn', block_rows, train_rows, preferred_element_type=jn...  11.4 us
  transfers between devices with their start and end apart: 6, of which 6 were waited for; matrix products, arithmetic and copies ran while one was open for 0% of the time, Pallas kernels for 0%

profile of v1, /device:TPU:0, one launch (start us, length us, event | category | flops | bytes accessed | tf_op | source)
XLA Modules:
  0.0 568.4 jit_solution(12359450322443537457)
XLA Ops:
  6.5 0.0 copy-start
  6.5 0.0 all-gather.2.cloned.1.call-start
  6.5 0.7 all-gather.2.cloned.1.call-update
  7.3 0.0 reduce-scatter.2.cloned.1.call-start
  8.0 0.7 add_divide_fusion
  8.6 0.1 dynamic_slice.3
  8.7 64.5 %all-gather.2.cloned.1.call-done = bf16[128,8192]{1,0:T(8,128)(2,1)} async-done(((bf16[8,8192]{1,0:T(8,128)(2,1)}), bf16[128,8192]{1,0:T(8,128)(2,1)}) %all-gather.2.cloned.1.call-update) | async-done | bytes 2097168 | tf_op jit(solution)/shard_map/all_gather | solution.py:15
  73.2 0.0 copy-done
  73.2 2.3 fusion.5
  75.5 3.6 psum.7
  79.1 1.8 fusion.2
  80.9 1.3 collective-permute-start
  82.3 91.5 %collective-permute-done = f32[128,8192]{1,0:T(8,128)S(1)} collective-permute-done((f32[128,8192]{1,0:T(8,128)S(1)}, f32[128,8192]{1,0:T(8,128)S(1)}, u32[]{:S(2)}, u32[]{:S(2)}) %collective-permute-start) | collective-permute-done | bytes 4194336 | tf_op jit(solution)/shard_map/ppermute | solution.py:26
  173.8 0.5 add.28
  174.3 1.5 collective-permute-start.1
  175.9 90.5 %collective-permute-done.1 = f32[128,8192]{1,0:T(8,128)S(1)} collective-permute-done((f32[128,8192]{1,0:T(8,128)S(1)}, f32[128,8192]{1,0:T(8,128)S(1)}, u32[]{:S(2)}, u32[]{:S(2)}) %collective-permute-start.1) | collective-permute-done | bytes 4194336 | tf_op jit(solution)/shard_map/ppermute | solution.py:26
  266.3 0.5 add.29
  266.9 0.0 copy-start.1
  266.9 1.5 collective-permute-start.2
  268.4 89.6 %collective-permute-done.2 = f32[128,8192]{1,0:T(8,128)S(1)} collective-permute-done((f32[128,8192]{1,0:T(8,128)S(1)}, f32[128,8192]{1,0:T(8,128)S(1)}, u32[]{:S(2)}, u32[]{:S(2)}) %collective-permute-start.2) | collective-permute-done | bytes 4194336 | tf_op jit(solution)/shard_map/ppermute | solution.py:26
  358.0 0.5 add.30
  358.6 1.7 collective-permute-start.3
  360.3 179.4 %collective-permute-done.3 = f32[128,8192]{1,0:T(8,128)S(1)} collective-permute-done((f32[128,8192]{1,0:T(8,128)S(1)}, f32[128,8192]{1,0:T(8,128)S(1)}, u32[]{:S(2)}, u32[]{:S(2)}) %collective-permute-start.3) | collective-permute-done | bytes 4194336 | tf_op jit(solution)/shard_map/ppermute | solution.py:26
  539.7 0.0 copy-start.2
  539.7 1.9 copy-done.2
  541.6 0.0 copy-done.1
  541.6 11.4 %fusion = f32[128,1024]{1,0:T(8,128)} fusion(bf16[1024,8192]{1,0:T(8,128)(2,1)} %param.9, f32[128,8192]{1,0:T(8,128)S(1)} %add.30, f32[128,8192]{1,0:T(8,128)} %copy-done.2, bf16[128,8192]{1,0:T(8,128)(2,1)S(1)} %copy-done.1, f32[]{:T(128)} %bitcast.6), kind=kOutput, calls=%fused_computation.1 | convolution fusion | flops 2152726528 | bytes 27787268 | tf_op jit(solution)/shard_map/qk,nk->qn/dot_general | solution.py:8
  553.0 0.0 reduce-scatter.2.cloned.1.call-update
  553.1 6.9 %reduce-scatter.2.cloned.1.call-done = f32[64,1024]{1,0:T(8,128)} async-done(((f32[128,1024]{1,0:T(8,128)}), f32[64,1024]{1,0:T(8,128)}) %reduce-scatter.2.cloned.1.call-update) | async-done | bytes 262160 | tf_op jit(solution)/shard_map/reduce_scatter | solution.py:32
  559.9 1.6 convert_element_type.12
Async XLA Ops:
  6.5 66.7 %copy-start = (bf16[8192,64]{0,1:T(8,128)(2,1)S(1)}, bf16[8192,64]{0,1:T(8,128)(2,1)}, u32[]{:S(2)}) copy-start(bf16[8192,64]{0,1:T(8,128)(2,1)} %param.6) | copy-start | bytes 3145732
  6.5 66.7 %all-gather.2.cloned.1.call-start = ((), (), s32[]{:S(2)}) async-start(), calls=%async_computation.1 | async-start | bytes 2228224 | tf_op jit(solution)/shard_map/all_gather | solution.py:15
  7.3 552.7 %reduce-scatter.2.cloned.1.call-start = ((), (), s32[]{:S(2)}) async-start(), calls=%async_computation.2 | async-start | bytes 786432 | tf_op jit(solution)/shard_map/reduce_scatter | solution.py:32
  80.9 92.9 %collective-permute-start = (f32[128,8192]{1,0:T(8,128)S(1)}, f32[128,8192]{1,0:T(8,128)S(1)}, u32[]{:S(2)}, u32[]{:S(2)}) collective-permute-start(f32[128,8192]{1,0:T(8,128)S(1)} %fusion.2), channel_id=1, source_target_pairs={{0,2},{2,0},{4,6},{6,4},{8,10},{10,8},{12,14},{14,12},{16,18},{18,... | collective-permute-start | bytes 12582920 | tf_op jit(solution)/shard_map/ppermute | solution.py:26
  174.3 92.0 %collective-permute-start.1 = (f32[128,8192]{1,0:T(8,128)S(1)}, f32[128,8192]{1,0:T(8,128)S(1)}, u32[]{:S(2)}, u32[]{:S(2)}) collective-permute-start(f32[128,8192]{1,0:T(8,128)S(1)} %add.28), channel_id=1, source_target_pairs={{0,4},{2,6},{4,0},{6,2},{8,12},{10,14},{12,8},{14,10},{16,20},{18,... | collective-permute-start | bytes 12582920 | tf_op jit(solution)/shard_map/ppermute | solution.py:26
  266.9 274.8 %copy-start.1 = (bf16[128,8192]{1,0:T(8,128)(2,1)S(1)}, bf16[128,8192]{1,0:T(8,128)(2,1)}, u32[]{:S(2)}) copy-start(bf16[128,8192]{1,0:T(8,128)(2,1)} %all-gather.2.cloned.1.call-done) | copy-start | bytes 6291460
  266.9 91.2 %collective-permute-start.2 = (f32[128,8192]{1,0:T(8,128)S(1)}, f32[128,8192]{1,0:T(8,128)S(1)}, u32[]{:S(2)}, u32[]{:S(2)}) collective-permute-start(f32[128,8192]{1,0:T(8,128)S(1)} %add.29), channel_id=1, source_target_pairs={{0,8},{2,10},{4,12},{6,14},{8,0},{10,2},{12,4},{14,6},{16,24},{18,... | collective-permute-start | bytes 12582920 | tf_op jit(solution)/shard_map/ppermute | solution.py:26
  358.6 181.1 %collective-permute-start.3 = (f32[128,8192]{1,0:T(8,128)S(1)}, f32[128,8192]{1,0:T(8,128)S(1)}, u32[]{:S(2)}, u32[]{:S(2)}) collective-permute-start(f32[128,8192]{1,0:T(8,128)S(1)} %add.30), channel_id=1, source_target_pairs={{0,16},{2,18},{4,20},{6,22},{8,24},{10,26},{12,28},{14,30},{16,0},... | collective-permute-start | bytes 12582920 | tf_op jit(solution)/shard_map/ppermute | solution.py:26
  539.7 1.9 copy-start.2
Sparse Core Ops, SparseCore 0:
  10.1 63.0 all-gather.1
  553.2 6.7 reduce-scatter.1
